TPU v7x, 32 devices: a whole 2x2x4 slice. The times are simulated.
32 devices in a mesh: batch: 4 (over y, x), seq: 4 (over z), head: 2 (over core).
Axes of the slice: x: 2, y: 2, z: 4, core: 2. Of those that a mesh axis runs over, the one named last changes fastest.
Arguments:
- hidden: bfloat16 [4, 2048, 1024], P('batch', 'seq', 'head'), may hold values from -6 to 6
- norm_gain: bfloat16 [1024], P('head'), may hold values from 0.099609375 to 1.8984375
- gate_weight: bfloat16 [1024, 2048], P(None, 'head'), may hold values from -0.1875 to 0.1875
- inner_weight: bfloat16 [1024, 2048], P(None, 'head'), may hold values from -0.1875 to 0.1875
- step_weight: bfloat16 [1024, 32], P(None, 'head'), may hold values from -0.375 to 0.375
- maps_weight: bfloat16 [1024, 256], replicated, may hold values from -0.1875 to 0.1875
- inner_kernel: float32 [4, 2048], P(None, 'head'), may hold values from -3 to 3
- inner_bias: float32 [2048], P('head'), may hold values from -1 to 1
- maps_kernel: float32 [4, 256], replicated, may hold values from -3 to 3
- maps_bias: float32 [256], replicated, may hold values from -1 to 1
- step_bias: float32 [32], P('head'), may hold values from -7 to -5
- decay_log: float32 [32], P('head'), may hold values from -5.3 to 1
- skip_gain: float32 [32], P('head'), may hold values from 1 to 4
- gate_gain: float32 [2048], P('head'), may hold values from 0.1 to 1.9
- output_weight: bfloat16 [2048, 1024], P('head'), may hold values from -0.125 to 0.125
- cotangent: bfloat16 [4, 2048, 1024], P('batch', 'seq', 'head'), may hold values from -6 to 6
Outputs:
- output: float32 [4, 2048, 1024], P('batch', 'seq', 'head')
- grad_hidden: float32 [4, 2048, 1024], P('batch', 'seq', 'head')
- grad_norm_gain: float32 [1024], P('head')
- grad_gate_weight: float32 [1024, 2048], P(None, 'head')
- grad_inner_weight: float32 [1024, 2048], P(None, 'head')
- grad_step_weight: float32 [1024, 32], P(None, 'head')
- grad_maps_weight: float32 [1024, 256], replicated
- grad_inner_kernel: float32 [4, 2048], P(None, 'head')
- grad_inner_bias: float32 [2048], P('head')
- grad_maps_kernel: float32 [4, 256], replicated
- grad_maps_bias: float32 [256], replicated
- grad_step_bias: float32 [32], P('head')
- grad_decay_log: float32 [32], P('head')
- grad_skip_gain: float32 [32], P('head')
- grad_gate_gain: float32 [2048], P('head')
- grad_output_weight: float32 [2048, 1024], P('head')
All inputs are finite; a program needn't handle non-finite values.
Results may differ from a plain program's by a relative error of at most 0.0089.
Values may be sent and summed in bfloat16 or wider, within the bound.
A program may use at most 192 MiB of HBM per device.

v0:
```python
import jax
import jax.numpy as jnp
from jax import lax
from jax.sharding import PartitionSpec as P

D = 1024
HEADDIM = 64
STATE = 128
CONV = 4
GROUP = 256
DI = 2048
HIGH = lax.Precision.HIGHEST
EPSILON = 1e-05


def shifted(array, axis, by):
    count = lax.axis_size(axis)
    pairs = [(i, i + by) for i in range(count) if 0 <= i + by < count]
    return lax.ppermute(array, axis, pairs)


def entering(array, axis, combine, identity, reverse):
    count, index = (lax.axis_size(axis), lax.axis_index(axis))
    everything = jax.tree.map(lambda part: lax.all_gather(part, axis), array)
    start = jax.tree.map(
        lambda part, zero: jnp.broadcast_to(jnp.asarray(zero, part.dtype), part.shape),
        array,
        identity,
    )

    def step(k, before):
        at = count - 1 - k if reverse else k
        reached = at > index if reverse else at < index
        new = combine(before, jax.tree.map(lambda part: part[at], everything))
        return jax.tree.map(lambda a, b: jnp.where(reached, a, b), new, before)

    return lax.fori_loop(0, count, step, start)


def silu_slope(values):
    sigmoid = jax.nn.sigmoid(values)
    return sigmoid * (1.0 + values * (1.0 - sigmoid))


def ssd_blocks(inner_act, write_map, read_map, step_size, decay_rates, initial):
    length, heads, headdim = inner_act.shape
    blocks_count = length // GROUP
    inner_blocks = inner_act.reshape(blocks_count, GROUP, heads, headdim)
    write_blocks = write_map.reshape(blocks_count, GROUP, write_map.shape[-1])
    read_blocks = read_map.reshape(blocks_count, GROUP, read_map.shape[-1])
    step_blocks = step_size.reshape(blocks_count, GROUP, heads)
    causal = (jnp.arange(GROUP)[:, None] >= jnp.arange(GROUP)[None, :])[:, :, None]

    def advance(state_in, pieces):
        inner_part, write_part, read_part, step_part = pieces
        cumlog = jnp.cumsum(step_part * decay_rates[None, :], axis=0)
        spread = jnp.where(causal, cumlog[:, None, :] - cumlog[None, :, :], 0.0)
        decays = jnp.where(causal, jnp.exp(spread), 0.0)
        scores = jnp.dot(read_part, write_part.T, precision=HIGH)
        weighted = inner_part * step_part[:, :, None]
        within = jnp.einsum("tsh,shp->thp", decays * scores[:, :, None], weighted, precision=HIGH)
        carried = jnp.einsum("tn,hpn->thp", read_part, state_in, precision=HIGH)
        result = within + jnp.exp(cumlog)[:, :, None] * carried
        remain = jnp.exp(cumlog[-1][None, :] - cumlog)
        fresh = jnp.einsum("shp,sn->hpn", weighted * remain[:, :, None], write_part, precision=HIGH)
        state_out = jnp.exp(cumlog[-1])[:, None, None] * state_in + fresh
        return (state_out, result)

    final, outputs = lax.scan(
        advance, initial, (inner_blocks, write_blocks, read_blocks, step_blocks)
    )
    return (outputs.reshape(length, heads, headdim), final)


def batched_scan(inner_heads, write_map, read_map, step_size, decay_rates, state_in):
    return jax.vmap(ssd_blocks, in_axes=(0, 0, 0, 0, None, 0))(
        inner_heads, write_map, read_map, step_size, decay_rates, state_in
    )


def chain_pair(earlier, later):
    return (earlier[0] * later[0], earlier[1] * later[0][:, :, None, None] + later[1])


def conv_apply(padded, kernel, bias_row, length):
    summed = bias_row
    for offset in range(kernel.shape[0]):
        summed = summed + kernel[offset] * padded[..., offset : offset + length, :]
    return summed


def conv_grads(padded, extended, grad_out, kernel, length):
    leading = tuple(range(grad_out.ndim - 1))
    grad_kernel = jnp.stack(
        [
            jnp.sum(grad_out * padded[..., offset : offset + length, :], axis=leading)
            for offset in range(kernel.shape[0])
        ]
    )
    grad_bias = jnp.sum(grad_out, axis=leading)
    width_less = kernel.shape[0] - 1
    grad_input = jnp.zeros_like(grad_out)
    for offset in range(kernel.shape[0]):
        begin_at = width_less - offset
        grad_input = grad_input + kernel[offset] * extended[..., begin_at : begin_at + length, :]
    return (grad_input, grad_kernel, grad_bias)


def on_device(
    hidden,
    norm_gain,
    gate_weight,
    inner_weight,
    step_weight,
    maps_weight,
    inner_kernel,
    inner_bias,
    maps_kernel,
    maps_bias,
    step_bias,
    decay_log,
    skip_gain,
    gate_gain,
    output_weight,
    cotangent,
):
    seq_count, tok_count, local_width = hidden.shape
    rows_count = seq_count * tok_count
    local_inner = gate_weight.shape[1]
    heads_local = step_weight.shape[1]
    whole_hidden, whole_cotangent, whole_gain = (
        lax.all_gather(hidden, "head", axis=2, tiled=True),
        lax.all_gather(cotangent, "head", axis=2, tiled=True),
        lax.all_gather(norm_gain, "head", axis=0, tiled=True),
    )
    residual = whole_hidden.reshape(rows_count, D).astype(jnp.float32)
    inverse = lax.rsqrt(jnp.mean(residual * residual, axis=-1, keepdims=True) + EPSILON)
    normal = residual * inverse
    normed = (normal * whole_gain.astype(jnp.float32)).astype(jnp.bfloat16)
    gate_pre = jnp.dot(normed, gate_weight, preferred_element_type=jnp.float32)
    inner_pre = jnp.dot(normed, inner_weight, preferred_element_type=jnp.float32)
    maps_pre = jnp.dot(normed, maps_weight, preferred_element_type=jnp.float32)
    step_pre = jnp.dot(normed, step_weight, preferred_element_type=jnp.float32).reshape(
        seq_count, tok_count, heads_local
    )
    inner_seq = inner_pre.reshape(seq_count, tok_count, local_inner)
    maps_seq = maps_pre.reshape(seq_count, tok_count, 2 * STATE)
    edge_inner, edge_maps = shifted(
        (inner_seq[:, tok_count - (CONV - 1) :, :], maps_seq[:, tok_count - (CONV - 1) :, :]),
        "seq",
        1,
    )
    inner_pad = jnp.concatenate([edge_inner, inner_seq], axis=1)
    maps_pad = jnp.concatenate([edge_maps, maps_seq], axis=1)
    inner_conv = conv_apply(inner_pad, inner_kernel, inner_bias, tok_count)
    maps_conv = conv_apply(maps_pad, maps_kernel, maps_bias, tok_count)
    inner_act = jax.nn.silu(inner_conv)
    maps_act = jax.nn.silu(maps_conv)
    write_map = maps_act[..., :STATE]
    read_map = maps_act[..., STATE:]
    step_size = jax.nn.softplus(step_pre + step_bias)
    decay_rates = -jnp.exp(decay_log)
    inner_heads = inner_act.reshape(seq_count, tok_count, heads_local, HEADDIM)
    zero_state = jnp.zeros((seq_count, heads_local, HEADDIM, STATE), jnp.float32)
    local_mix, local_state = batched_scan(
        inner_heads, write_map, read_map, step_size, decay_rates, zero_state
    )
    cumlog = jnp.cumsum(step_size * decay_rates, axis=1)
    total_decay = jnp.exp(cumlog[:, -1, :])
    identity = (jnp.ones_like(total_decay), jnp.zeros_like(local_state))
    prefix_decay, state_in = entering(
        (total_decay, local_state), "seq", chain_pair, identity, False
    )
    carried = jnp.einsum("stn,shpn->sthp", read_map, state_in, precision=HIGH)
    mixed_out = (
        local_mix
        + jnp.exp(cumlog)[..., None] * carried
        + skip_gain[None, None, :, None] * inner_heads
    )
    mixed_flat = mixed_out.reshape(rows_count, local_inner)
    gate_act = jax.nn.silu(gate_pre)
    gated_val = mixed_flat * gate_act
    square_total = lax.psum(jnp.sum(gated_val * gated_val, axis=-1), "head")
    scale_back = lax.rsqrt(square_total[:, None] / DI + EPSILON)
    gated_norm = (gated_val * scale_back * gate_gain).astype(jnp.bfloat16)
    branch_part = jnp.dot(gated_norm, output_weight, preferred_element_type=jnp.float32)
    branch = lax.psum_scatter(branch_part, "head", scatter_dimension=1, tiled=True)
    output = (hidden.reshape(rows_count, local_width).astype(jnp.float32) + branch).reshape(
        seq_count, tok_count, local_width
    )
    cot_rows = whole_cotangent.reshape(rows_count, D)
    grad_output_weight = jnp.dot(gated_norm.T, cot_rows, preferred_element_type=jnp.float32)
    grad_norm_out = jnp.dot(cot_rows, output_weight.T, preferred_element_type=jnp.float32)
    grad_gate_gain = jnp.sum(grad_norm_out * gated_val * scale_back, axis=0)
    grad_scaled = grad_norm_out * gate_gain
    dot_total = lax.psum(jnp.sum(grad_scaled * gated_val, axis=-1), "head")
    grad_gated = scale_back * (
        grad_scaled - gated_val * scale_back * scale_back * (dot_total[:, None] / DI)
    )
    grad_mixed = (grad_gated * gate_act).reshape(seq_count, tok_count, heads_local, HEADDIM)
    grad_gate_pre = grad_gated * mixed_flat * silu_slope(gate_pre)
    grad_skip_gain = jnp.sum(grad_mixed * inner_heads, axis=(0, 1, 3))
    from_here = jnp.einsum(
        "sthp,stn->shpn", grad_mixed * jnp.exp(cumlog)[..., None], read_map, precision=HIGH
    )
    suffix_decay, state_grad = entering((total_decay, from_here), "seq", chain_pair, identity, True)
    recomputed, scan_back = jax.vjp(
        batched_scan, inner_heads, write_map, read_map, step_size, decay_rates, state_in
    )
    grad_inner_heads, grad_write, grad_read, grad_step, grad_rates, grad_start = scan_back(
        (grad_mixed, state_grad)
    )
    grad_write, grad_read = lax.psum((grad_write, grad_read), "head")
    grad_maps = jnp.concatenate([grad_write, grad_read], axis=-1)
    grad_inner = (grad_inner_heads + skip_gain[None, None, :, None] * grad_mixed).reshape(
        seq_count, tok_count, local_inner
    )
    grad_inner_conv = grad_inner * silu_slope(inner_conv)
    grad_maps_conv = grad_maps * silu_slope(maps_conv)
    next_inner, next_maps = shifted(
        (grad_inner_conv[:, : CONV - 1, :], grad_maps_conv[:, : CONV - 1, :]), "seq", -1
    )
    inner_ext = jnp.concatenate([grad_inner_conv, next_inner], axis=1)
    maps_ext = jnp.concatenate([grad_maps_conv, next_maps], axis=1)
    grad_inner_pre, grad_inner_kernel, grad_inner_bias = conv_grads(
        inner_pad, inner_ext, grad_inner_conv, inner_kernel, tok_count
    )
    grad_maps_pre, grad_maps_kernel, grad_maps_bias = conv_grads(
        maps_pad, maps_ext, grad_maps_conv, maps_kernel, tok_count
    )
    grad_step_pre = grad_step * jax.nn.sigmoid(step_pre + step_bias)
    grad_step_bias = jnp.sum(grad_step_pre, axis=(0, 1))
    grad_decay_log = grad_rates * decay_rates
    gate_round = grad_gate_pre.astype(jnp.bfloat16)
    inner_round = grad_inner_pre.reshape(rows_count, local_inner).astype(jnp.bfloat16)
    maps_round = grad_maps_pre.reshape(rows_count, 2 * STATE).astype(jnp.bfloat16)
    step_round = grad_step_pre.reshape(rows_count, heads_local).astype(jnp.bfloat16)
    grad_gate_weight = jnp.dot(normed.T, gate_round, preferred_element_type=jnp.float32)
    grad_inner_weight = jnp.dot(normed.T, inner_round, preferred_element_type=jnp.float32)
    grad_maps_weight = jnp.dot(normed.T, maps_round, preferred_element_type=jnp.float32)
    grad_step_weight = jnp.dot(normed.T, step_round, preferred_element_type=jnp.float32)
    partial_normed = jnp.dot(gate_round, gate_weight.T, preferred_element_type=jnp.float32)
    partial_normed = partial_normed + jnp.dot(
        inner_round, inner_weight.T, preferred_element_type=jnp.float32
    )
    partial_normed = partial_normed + jnp.dot(
        step_round, step_weight.T, preferred_element_type=jnp.float32
    )
    input_share = lax.psum_scatter(partial_normed, "head", scatter_dimension=1, tiled=True)
    column_start = lax.axis_index("head") * local_width
    maps_rows = lax.dynamic_slice_in_dim(maps_weight, column_start, local_width, 0)
    input_share = input_share + jnp.dot(maps_round, maps_rows.T, preferred_element_type=jnp.float32)
    normal_local = lax.dynamic_slice_in_dim(normal, column_start, local_width, 1)
    grad_normal = input_share * norm_gain.astype(jnp.float32)
    dot_sum = lax.psum(jnp.sum(grad_normal * normal_local, axis=-1), "head")
    grad_rows = inverse * (grad_normal - normal_local * (dot_sum[:, None] / D)) + cotangent.reshape(
        rows_count, local_width
    ).astype(jnp.float32)
    grad_hidden = grad_rows.reshape(seq_count, tok_count, local_width)
    grad_norm_gain = jnp.sum(input_share * normal_local, axis=0)
    summed = lax.psum(
        (
            grad_norm_gain,
            grad_gate_weight,
            grad_inner_weight,
            grad_step_weight,
            grad_maps_weight,
            grad_inner_kernel,
            grad_inner_bias,
            grad_maps_kernel,
            grad_maps_bias,
            grad_step_bias,
            grad_decay_log,
            grad_skip_gain,
            grad_gate_gain,
            grad_output_weight,
        ),
        ("batch", "seq"),
    )
    return (
        output,
        grad_hidden,
        summed[0],
        summed[1],
        summed[2],
        summed[3],
        summed[4],
        summed[5],
        summed[6],
        summed[7],
        summed[8],
        summed[9],
        summed[10],
        summed[11],
        summed[12],
        summed[13],
    )


def solution(mesh):
    return jax.shard_map(
        on_device,
        mesh=mesh,
        in_specs=(
            P("batch", "seq", "head"),
            P("head"),
            P(None, "head"),
            P(None, "head"),
            P(None, "head"),
            P(),
            P(None, "head"),
            P("head"),
            P(),
            P(),
            P("head"),
            P("head"),
            P("head"),
            P("head"),
            P("head", None),
            P("batch", "seq", "head"),
        ),
        out_specs=(
            P("batch", "seq", "head"),
            P("batch", "seq", "head"),
            P("head"),
            P(None, "head"),
            P(None, "head"),
            P(None, "head"),
            P(),
            P(None, "head"),
            P("head"),
            P(),
            P(),
            P("head"),
            P("head"),
            P("head"),
            P("head"),
            P("head", None),
        ),
        check_vma=False,
    )
```

profile of v0, /device:TPU:0, one launch (start us, length us, event | category | flops | bytes accessed | tf_op | source)
XLA Modules:
  0.0 855.7 jit_solution(2560668838805555344)
XLA Ops:
  13.6 7.7 all-gather.8.cloned.1.call-done
  50.1 70.7 %while.120 = (s32[]{:T(128)}, f32[1,16,64,128]{3,2,1,0:T(8,128)}, f32[2,1,256,16,64]{2,0,4,3,1:T(2,128)}, f32[2,1,256,16]{2,0,3,1:T(2,128)}, f32[16]{0:T(128)S(1...) while((s32[]{:T(128)}, f32[1,16,64,128]{3,2,1,0:T(8,128)}, ...), condition=%wide.region_4.5_spmd.clone.clone, body=%wide.region_1.4_spmd.clone.clone.sunk | while | flops 1717903360 | bytes 23170916 | solution.py:69
  53.6 4.8 fusion.317
  59.5 21.9 %dynamic_update_slice.235 = f32[2,1,256,16,64]{2,0,4,3,1:T(2,128)} dynamic-update-slice(f32[2,1,256,16,64]{2,0,4,3,1:T(2,128)} %get-tuple-element.2732, f32[1,1,256,16,64]{2,0,4,3,1:T(1,128)S(1)} %copy.413, s32[]{:T(128)} %get-tuple-element.2730, s32[]{:T(128)} %constant.258.clone.1..sunk.3, s32[]{:T(128)} %constant.258.clone.1..sunk.3, s32[]{:T(128)} %constant.258.clone.1..sunk.3, ...) | dynamic-update-slice | bytes 2097156 | tf_op jit(solution)/shard_map/vmap()/while/body/jit(dynamic_update_index_in_dim)/dynamic_update_slice | solution.py:69
  89.4 4.8 fusion.317
  95.3 21.9 %dynamic_update_slice.235 = f32[2,1,256,16,64]{2,0,4,3,1:T(2,128)} dynamic-update-slice(f32[2,1,256,16,64]{2,0,4,3,1:T(2,128)} %get-tuple-element.2732, f32[1,1,256,16,64]{2,0,4,3,1:T(1,128)S(1)} %copy.413, s32[]{:T(128)} %get-tuple-element.2730, s32[]{:T(128)} %constant.258.clone.1..sunk.3, s32[]{:T(128)} %constant.258.clone.1..sunk.3, s32[]{:T(128)} %constant.258.clone.1..sunk.3, ...) | dynamic-update-slice | bytes 2097156 | tf_op jit(solution)/shard_map/vmap()/while/body/jit(dynamic_update_index_in_dim)/dynamic_update_slice | solution.py:69
  124.2 9.4 %all_gather.29 = f32[4,1,16]{2,1,0:T(1,128)S(1)} all-gather(f32[1,1,16]{2,1,0:T(1,128)S(1)} %exp.133), channel_id=1, replica_groups=mesh['batch'=4,'seq'=4,'head'=2] {'seq'}, dimensions={0}, use_global_device_ids=true | all-gather | bytes 320 | tf_op jit(solution)/shard_map/all_gather | solution.py:24
  141.9 24.1 %all-gather.12.cloned.1.call-done = f32[4,16,64,128]{3,2,1,0:T(8,128)} async-done(((f32[1,16,64,128]{3,2,1,0:T(8,128)}), f32[4,16,64,128]{3,2,1,0:T(8,128)}) %all-gather.12.cloned.1.call-update) | async-done | bytes 2097168 | tf_op jit(solution)/shard_map/all_gather | solution.py:24
  166.0 4.8 while.118
  180.4 5.5 multiply_reduce_fusion.6
  188.5 5.9 multiply_reduce_fusion
  196.8 6.6 fusion.168
  220.1 46.4 %while.117 = (s32[]{:T(128)}, f32[1,16,64,128]{3,2,1,0:T(8,128)S(1)}, f32[2,1,256,256,16]{3,4,2,1,0:T(8,128)}, f32[2,1,128,256]{2,3,1,0:T(8,128)}, f32[2,1,256,1...) while((s32[]{:T(128)}, ...), condition=%wide.region_19.20_spmd.clone.clone, body=%wide.region_16.19_spmd.clone.clone.sunk | while | flops 912007232 | bytes 91645848 | solution.py:69
  225.2 6.3 multiply_dynamic-update-slice_fusion.4
  248.4 6.3 multiply_dynamic-update-slice_fusion.4
  271.0 4.5 copy.251
  275.5 7.3 while.119
  286.5 108.7 %while.121 = (s32[]{:T(128)}, f32[16]{0:T(128)}, f32[1,16,64,128]{3,2,1,0:T(8,128)S(1)}, f32[2,1,256,16,64]{2,4,3,1,0:T(8,128)}, f32[2,1,256,128]{3,2,1,0:T(8,12...) while((s32[]{:T(128)}, f32[16]{0:T(128)}, ...), condition=%wide.region_32.33_spmd.clone.clone, body=%wide.region_20.32_spmd.clone.clone.sunk | while | flops 3434913792 | bytes 128363696 | solution.py:69
  286.7 6.7 constant_dynamic-slice_fusion.20
  295.7 11.3 %fusion.331 = (f32[256,16]{0,1:T(8,128)}, f32[256,16]{0,1:T(8,128)}, f32[256,256]{1,0:T(8,128)S(1)}) fusion(f32[1,1,256,256,16]{3,4,2,1,0:T(8,128)S(1)} %constant_dynamic-slice_fusion.23, f32[256,256]{1,0:T(8,128)S(1)} %dynamic-slice_bitcast_fusion.8, pred[256,256]{1,0:T(8,128)(4,1)S(1)} %get-tuple-element.2976, ...), kind=kOutput, calls=%fused_computation.161.clone.1 | convolution fusion | flops 813621248 | bytes 11109376 | tf_op jit(solution)/shard_map/transpose(jvp(vmap()))/while/body/eval_jaxpr/tsh,shp->thp/dot_general | solution.py:61
  317.5 8.9 %fusion.330 = (f32[256,16]{0,1:T(8,128)S(1)}, f32[1,256,16,64]{1,3,2,0:T(8,128)}) fusion(f32[2,1,256,16,64]{2,4,3,1,0:T(8,128)} %get-tuple-element.2974, s32[]{:T(128)S(6)} %sub.235, f32[1,1,256,256,16]{3,4,2,1,0:T(8,128)} %get-tuple-element.2704, f32[2,1,256,16,64]{2,4,3,1,0:T(8,128)} %get-tuple-element.2960, ...), kind=kOutput, calls=%fused_computation.139.clone.1 | convolution fusion | flops 806350848 | bytes 8422400 | tf_op jit(solution)/shard_map/transpose(jvp(vmap()))/while/body/eval_jaxpr/tsh,shp->thp/dot_general | solution.py:61
  340.8 6.7 constant_dynamic-slice_fusion.20
  349.9 11.3 %fusion.331 = (f32[256,16]{0,1:T(8,128)}, f32[256,16]{0,1:T(8,128)}, f32[256,256]{1,0:T(8,128)S(1)}) fusion(f32[1,1,256,256,16]{3,4,2,1,0:T(8,128)S(1)} %constant_dynamic-slice_fusion.23, f32[256,256]{1,0:T(8,128)S(1)} %dynamic-slice_bitcast_fusion.8, pred[256,256]{1,0:T(8,128)(4,1)S(1)} %get-tuple-element.2976, ...), kind=kOutput, calls=%fused_computation.161.clone.1 | convolution fusion | flops 813621248 | bytes 11109376 | tf_op jit(solution)/shard_map/transpose(jvp(vmap()))/while/body/eval_jaxpr/tsh,shp->thp/dot_general | solution.py:61
  371.6 8.9 %fusion.330 = (f32[256,16]{0,1:T(8,128)S(1)}, f32[1,256,16,64]{1,3,2,0:T(8,128)}) fusion(f32[2,1,256,16,64]{2,4,3,1,0:T(8,128)} %get-tuple-element.2974, s32[]{:T(128)S(6)} %sub.235, f32[1,1,256,256,16]{3,4,2,1,0:T(8,128)} %get-tuple-element.2704, f32[2,1,256,16,64]{2,4,3,1,0:T(8,128)} %get-tuple-element.2960, ...), kind=kOutput, calls=%fused_computation.139.clone.1 | convolution fusion | flops 806350848 | bytes 8422400 | tf_op jit(solution)/shard_map/transpose(jvp(vmap()))/while/body/eval_jaxpr/tsh,shp->thp/dot_general | solution.py:61
  395.2 4.9 fusion.214
  404.0 4.9 copy.266
  408.8 4.9 reshape.1301
  413.8 6.4 fusion.222
  431.7 4.8 fusion.218
  462.0 81.9 %all-reduce.2 = (f32[512]{0:T(512)}, f32[4,1024]{1,0:T(4,128)}, f32[1024]{0:T(1024)}, f32[4,256]{1,0:T(4,128)}, f32[256]{0:T(256)}, /*index=5*/f32[16]{0:T(128)}, f32[16]{0:T(128)}, f32[16]{0:T(128)}, f32[1024]{0:T(1024)}) all-reduce(f32[512]{0:T(512)S(1)} %get-tuple-element.1965, ...), channel_id=1, replica_groups=mesh['batch'=4,'seq'=4,'head'=2] {'batch','seq'}, use_global_device_ids=true, to_apply=%region_39.40 | all-reduce | flops 7984 | bytes 63872 | tf_op jit(solution)/shard_map/psum | solution.py:261
  546.9 290.1 %all-reduce.8.cloned.1.call-done = (f32[1024,1024]{1,0:T(8,128)}, f32[1024,1024]{1,0:T(8,128)}, f32[1024,16]{0,1:T(8,128)}, f32[1024,256]{1,0:T(8,128)}, f32[1024,1024]{1,0:T(8,128)}) async-done(((f32[1024,1024]{1,0:T(8,128)}, f32[1024,1024]{1,0:T(8,128)}, f32[1024,16]{0,1:T(8,128)}, f32[1024,256]{1,0:T(8,128)}, f32[1024,1024]{1,0:T(8,128)}), (f32[1024,1024]{1,0:T(8,128)}, f32[1024,1024]{1,0:T(8,128)}, ...) | async-done | bytes 13697040 | tf_op jit(solution)/shard_map/psum | solution.py:261
  837.0 4.9 copy.557
  (611 shorter events, 252.2 us)
Async XLA Ops:
  7.2 173.2 %copy-start = (bf16[1024,1024]{1,0:T(8,128)(2,1)S(1)}, bf16[1024,1024]{1,0:T(8,128)(2,1)}, u32[]{:S(2)}) copy-start(bf16[1024,1024]{1,0:T(8,128)(2,1)} %param.28) | copy-start | bytes 6291460
  7.2 14.1 %all-gather.8.cloned.1.call-start = ((), (), s32[]{:S(2)}) async-start(), calls=%async_computation.2 | async-start | bytes 1572864 | tf_op jit(solution)/shard_map/all_gather | solution.py:132
  7.9 158.0 %all-gather.12.cloned.1.call-start = ((), (), s32[]{:S(2)}) async-start(), calls=%async_computation.6 | async-start | bytes 2621440 | tf_op jit(solution)/shard_map/all_gather | solution.py:24
  10.7 169.8 %copy-start.55 = (f32[2,1,512]{2,1,0:T(1,128)}, f32[2,1,512]{2,1,0:T(1,128)S(1)}, u32[]{:S(2)}) copy-start(f32[2,1,512]{2,1,0:T(1,128)S(1)} %convert_element_type.86) | copy-start | bytes 12292
  12.7 23.3 %copy-start.85 = (f32[1,256]{1,0:T(1,128)}, f32[1,256]{1,0:T(1,128)S(1)}, u32[]{:S(2)}) copy-start(f32[1,256]{1,0:T(1,128)S(1)} %get-tuple-element.2197) | copy-start | bytes 3076
  12.7 23.3 %copy-start.87 = (f32[1,256]{1,0:T(1,128)}, f32[1,256]{1,0:T(1,128)S(1)}, u32[]{:S(2)}) copy-start(f32[1,256]{1,0:T(1,128)S(1)} %get-tuple-element.2198) | copy-start | bytes 3076
  12.7 23.3 %copy-start.89 = (f32[1,256]{1,0:T(1,128)}, f32[1,256]{1,0:T(1,128)S(1)}, u32[]{:S(2)}) copy-start(f32[1,256]{1,0:T(1,128)S(1)} %get-tuple-element.2199) | copy-start | bytes 3076
  12.7 23.3 %copy-start.91 = (f32[1,256]{1,0:T(1,128)}, f32[1,256]{1,0:T(1,128)S(1)}, u32[]{:S(2)}) copy-start(f32[1,256]{1,0:T(1,128)S(1)} %get-tuple-element.2200) | copy-start | bytes 3076
  13.6 23.6 %copy-start.68 = (f32[1,1024]{1,0:T(1,128)}, f32[1,1024]{1,0:T(1,128)S(1)}, u32[]{:S(2)}) copy-start(f32[1,1024]{1,0:T(1,128)S(1)} %get-tuple-element.2193) | copy-start | bytes 12292
  13.6 23.6 %copy-start.70 = (f32[1,1024]{1,0:T(1,128)}, f32[1,1024]{1,0:T(1,128)S(1)}, u32[]{:S(2)}) copy-start(f32[1,1024]{1,0:T(1,128)S(1)} %get-tuple-element.2194) | copy-start | bytes 12292
  13.6 23.6 %copy-start.72 = (f32[1,1024]{1,0:T(1,128)}, f32[1,1024]{1,0:T(1,128)S(1)}, u32[]{:S(2)}) copy-start(f32[1,1024]{1,0:T(1,128)S(1)} %get-tuple-element.2195) | copy-start | bytes 12292
  13.6 23.6 %copy-start.74 = (f32[1,1024]{1,0:T(1,128)}, f32[1,1024]{1,0:T(1,128)S(1)}, u32[]{:S(2)}) copy-start(f32[1,1024]{1,0:T(1,128)S(1)} %get-tuple-element.2196) | copy-start | bytes 12292
  23.0 157.4 %copy-start.63 = (f32[512]{0:T(512)}, f32[512]{0:T(512)S(1)}, u32[]{:S(2)}) copy-start(f32[512]{0:T(512)S(1)} %add_rsqrt_fusion.1) | copy-start | bytes 6148
  24.9 11.1 %copy-start.30 = (f32[512,256]{1,0:T(8,128)}, f32[512,256]{1,0:T(8,128)S(1)}, u32[]{:S(2)}) copy-start(f32[512,256]{1,0:T(8,128)S(1)} %fusion.220) | copy-start | bytes 1572868
  24.9 9.9 %copy-start.76 = (bf16[1024,16]{0,1:T(8,128)(2,1)S(1)}, bf16[1024,16]{0,1:T(8,128)(2,1)}, u32[]{:S(2)}) copy-start(bf16[1024,16]{0,1:T(8,128)(2,1)} %param.30) | copy-start | bytes 98308
  24.9 9.9 %copy-start.100 = (f32[16]{0:T(128)S(1)}, f32[16]{0:T(128)}, u32[]{:S(2)}) copy-start(f32[16]{0:T(128)} %param.36) | copy-start | bytes 196
  24.9 11.0 %collective-permute-start.1 = (f32[1,3,256]{2,1,0:T(4,128)S(1)}, f32[1,3,256]{2,1,0:T(4,128)S(1)}, u32[]{:S(2)}, u32[]{:S(2)}) collective-permute-start(f32[1,3,256]{2,1,0:T(4,128)S(1)} %slice.201), channel_id=1, source_target_pairs={{0,2},{2,4},{4,6},{1,3},{3,5},{5,7},{8,10},{10,12},{12,14},{9,11},... | collective-permute-start | bytes 9224 | tf_op jit(solution)/shard_map/ppermute | solution.py:19
  31.4 5.8 collective-permute-start
  120.8 67.6 %all-gather.10.cloned.1.call-start = ((), (), s32[]{:S(2)}) async-start(), calls=%async_computation.4 | async-start | bytes 1572864 | tf_op jit(solution)/shard_map/all_gather | solution.py:133
  121.6 154.0 %all-gather.14.cloned.1.call-start = ((), (), s32[]{:S(2)}) async-start(), calls=%async_computation.7 | async-start | bytes 2621440 | tf_op jit(solution)/shard_map/all_gather | solution.py:24
  180.4 8.0 copy-start.61
  188.4 8.4 copy-start.78
  213.6 227.5 %all-reduce.10.cloned.1.call-start = ((), (), s32[]{:S(2)}) async-start(), calls=%async_computation.9 | async-start | bytes 1048576 | tf_op jit(solution)/shard_map/psum | solution.py:213
  317.5 13.2 %copy-start.57 = (f32[2,1,256,16,1]{2,0,4,3,1:T(2,128)S(1)}, f32[2,1,256,16,1]{2,0,4,3,1:T(2,128)}, u32[]{:S(2)}) copy-start(f32[2,1,256,16,1]{2,0,4,3,1:T(2,128)} %get-tuple-element.2966) | copy-start | bytes 98308 | tf_op jit(solution)/shard_map/transpose(jvp(vmap()))/while
  371.6 13.2 %copy-start.57 = (f32[2,1,256,16,1]{2,0,4,3,1:T(2,128)S(1)}, f32[2,1,256,16,1]{2,0,4,3,1:T(2,128)}, u32[]{:S(2)}) copy-start(f32[2,1,256,16,1]{2,0,4,3,1:T(2,128)} %get-tuple-element.2966) | copy-start | bytes 98308 | tf_op jit(solution)/shard_map/transpose(jvp(vmap()))/while
  395.2 58.2 %reduce-scatter.3.cloned.1.call-start = ((), (), s32[]{:S(2)}) async-start(), calls=%async_computation.3 | async-start | bytes 3145728 | tf_op jit(solution)/shard_map/reduce_scatter | solution.py:187
  400.2 55.8 %reduce-scatter.5.cloned.1.call-start = ((), (), s32[]{:S(2)}) async-start(), calls=%async_computation.5 | async-start | bytes 3145728 | tf_op jit(solution)/shard_map/reduce_scatter | solution.py:249
  413.8 8.0 copy-start.77
  420.3 5.6 collective-permute-start.2
  430.5 406.5 %all-reduce.8.cloned.1.call-start = ((), (), s32[]{:S(2)}) async-start(), calls=%async_computation.8 | async-start | bytes 27394048 | tf_op jit(solution)/shard_map/psum | solution.py:261
  443.6 5.5 collective-permute-start.3
  455.9 88.0 %copy-start.35 = (f32[512,512]{1,0:T(8,128)S(1)}, f32[512,512]{1,0:T(8,128)}, u32[]{:S(2)}) copy-start(f32[512,512]{1,0:T(8,128)} %reduce-scatter.5.cloned.1.call-done) | copy-start | bytes 3145732
  (124 other events, 505.1 us)
Sparse Core Ops, SparseCore 0:
  9.5 11.7 all-gather.7
  121.0 44.9 all-gather.11
  167.5 7.8 all-gather.9
  213.7 44.5 all-gather.13
  395.3 17.5 all-reduce.9
  415.0 10.8 reduce-scatter.2
  430.6 8.5 reduce-scatter.4
  451.1 385.9 all-reduce.7
where the time goes:
time: 872 us; the launch traced here: 856 us
  waiting for transfers between devices  328 us (38%)
  local copies, waits for them, and re-layouts  169 us (19%)
  matrix products  141 us (16%)
  blocking collectives  101 us (12%)
  other arithmetic  90.1 us (10%)
  between operations  15.5 us (2%)
  starting transfers between devices  10.8 us (1%)
    psum x1, waiting for transfers between devices, on_device(): lax.psum((grad_norm_gain, grad_gate_weight, grad_inner_weight, grad_step_...  290 us
    psum x1, blocking collectives, on_device(): lax.psum((grad_norm_gain, grad_gate_weight, grad_inner_weight, grad_step_...  81.9 us
    dynamic_update_slice x24, local copies, waits for them, and re-layouts, ssd_blocks(): lax.scan(advance, initial, (inner_blocks, write_blocks, read_blocks, step...  63.8 us
    dot_general x6, matrix products, advance(): jnp.einsum('tsh,shp->thp', decays * scores[:, :, None], weighted, precisi...  50 us
    unnamed x150, local copies, waits for them, and re-layouts  26.9 us
    all_gather x2, waiting for transfers between devices, entering(): everything = jax.tree.map(lambda part: lax.all_gather(part, axis), array)  24.1 us
    dynamic_slice x18, local copies, waits for them, and re-layouts, ssd_blocks(): lax.scan(advance, initial, (inner_blocks, write_blocks, read_blocks, step...  17.4 us
  transfers between devices with their start and end apart: 12, of which 5 were waited for; matrix products, arithmetic and copies ran while one was open for 18% of the time, Pallas kernels for 0%

commit v1 on v0

--- a/solution.py
+++ b/solution.py
@@ -259,23 +259,26 @@
     grad_hidden = grad_rows.reshape(seq_count, tok_count, local_width)
     grad_norm_gain = jnp.sum(input_share * normal_local, axis=0)
     summed = lax.psum(
-        (
-            grad_norm_gain,
-            grad_gate_weight,
-            grad_inner_weight,
-            grad_step_weight,
-            grad_maps_weight,
-            grad_inner_kernel,
-            grad_inner_bias,
-            grad_maps_kernel,
-            grad_maps_bias,
-            grad_step_bias,
-            grad_decay_log,
-            grad_skip_gain,
-            grad_gate_gain,
-            grad_output_weight,
+        lax.psum(
+            (
+                grad_norm_gain,
+                grad_gate_weight,
+                grad_inner_weight,
+                grad_step_weight,
+                grad_maps_weight,
+                grad_inner_kernel,
+                grad_inner_bias,
+                grad_maps_kernel,
+                grad_maps_bias,
+                grad_step_bias,
+                grad_decay_log,
+                grad_skip_gain,
+                grad_gate_gain,
+                grad_output_weight,
+            ),
+            "batch",
         ),
-        ("batch", "seq"),
+        "seq",
     )
     return (
         output,

time: 872 us -> 1240 us (1.42)
  waiting for transfers between devices: 328 us -> 734 us
  blocking collectives: 101 us -> 58.9 us
    psum x0 -> x1, waiting for transfers between devices: none -> 419 us  [on_device(): lax.psum(lax.psum((grad_norm_gain, grad_gate_weight, grad_inner_weight, g...]
    psum x1, blocking collectives: 81.9 us -> 17 us  [on_device(): lax.psum((grad_norm_gain, grad_gate_weight, grad_inner_weight, grad_step_...]
    psum x1, waiting for transfers between devices: 290 us -> 247 us  [on_device(): lax.psum((grad_norm_gain, grad_gate_weight, grad_inner_weight, grad_step_...]
    psum x0 -> x1, blocking collectives: none -> 23.3 us  [on_device(): lax.psum(lax.psum((grad_norm_gain, grad_gate_weight, grad_inner_weight, g...]
    unnamed x150 -> x152, local copies, waits for them, and re-layouts: 26.9 us -> 26.5 us
  transfers between devices with their start and end apart: 12 -> 13, of which waited for: 5 -> 9; matrix products, arithmetic and copies ran while one was open for 18% -> 11% of each run, Pallas kernels for 0% -> 0%
where the time goes in v1:
time: 1240 us; the launch traced here: 1220 us
  waiting for transfers between devices  734 us (59%)
  local copies, waits for them, and re-layouts  171 us (14%)
  matrix products  140 us (11%)
  other arithmetic  91.5 us (7%)
  blocking collectives  58.9 us (5%)
  between operations  15.2 us (1%)
    psum x1, waiting for transfers between devices, on_device(): lax.psum(lax.psum((grad_norm_gain, grad_gate_weight, grad_inner_weight, g...  419 us
    psum x1, waiting for transfers between devices, on_device(): lax.psum((grad_norm_gain, grad_gate_weight, grad_inner_weight, grad_step_...  247 us
    dynamic_update_slice x24, local copies, waits for them, and re-layouts, ssd_blocks(): lax.scan(advance, initial, (inner_blocks, write_blocks, read_blocks, step...  63.8 us
    dot_general x6, matrix products, advance(): jnp.einsum('tsh,shp->thp', decays * scores[:, :, None], weighted, precisi...  50 us
    unnamed x152, local copies, waits for them, and re-layouts  26.5 us
  transfers between devices with their start and end apart: 13, of which 9 were waited for; matrix products, arithmetic and copies ran while one was open for 11% of the time, Pallas kernels for 0%

profile of v1, /device:TPU:0, one launch (start us, length us, event | category | flops | bytes accessed | tf_op | source)
XLA Modules:
  0.0 1222.9 jit_solution(11248333143010310421)
XLA Ops:
  13.6 7.7 all-gather.8.cloned.1.call-done
  50.0 70.7 %while.120 = (s32[]{:T(128)}, f32[1,16,64,128]{3,2,1,0:T(8,128)}, f32[2,1,256,16,64]{2,0,4,3,1:T(2,128)}, f32[2,1,256,16]{2,0,3,1:T(2,128)}, f32[16]{0:T(128)S(1...) while((s32[]{:T(128)}, f32[1,16,64,128]{3,2,1,0:T(8,128)}, ...), condition=%wide.region_4.5_spmd.clone.clone, body=%wide.region_1.4_spmd.clone.clone.sunk | while | flops 1717903360 | bytes 23170916 | solution.py:69
  59.4 21.9 %dynamic_update_slice.235 = f32[2,1,256,16,64]{2,0,4,3,1:T(2,128)} dynamic-update-slice(f32[2,1,256,16,64]{2,0,4,3,1:T(2,128)} %get-tuple-element.2746, f32[1,1,256,16,64]{2,0,4,3,1:T(1,128)S(1)} %copy.413, s32[]{:T(128)} %get-tuple-element.2744, s32[]{:T(128)} %constant.258.clone.1..sunk.3, s32[]{:T(128)} %constant.258.clone.1..sunk.3, s32[]{:T(128)} %constant.258.clone.1..sunk.3, ...) | dynamic-update-slice | bytes 2097156 | tf_op jit(solution)/shard_map/vmap()/while/body/jit(dynamic_update_index_in_dim)/dynamic_update_slice | solution.py:69
  95.2 21.9 %dynamic_update_slice.235 = f32[2,1,256,16,64]{2,0,4,3,1:T(2,128)} dynamic-update-slice(f32[2,1,256,16,64]{2,0,4,3,1:T(2,128)} %get-tuple-element.2746, f32[1,1,256,16,64]{2,0,4,3,1:T(1,128)S(1)} %copy.413, s32[]{:T(128)} %get-tuple-element.2744, s32[]{:T(128)} %constant.258.clone.1..sunk.3, s32[]{:T(128)} %constant.258.clone.1..sunk.3, s32[]{:T(128)} %constant.258.clone.1..sunk.3, ...) | dynamic-update-slice | bytes 2097156 | tf_op jit(solution)/shard_map/vmap()/while/body/jit(dynamic_update_index_in_dim)/dynamic_update_slice | solution.py:69
  124.8 9.3 all_gather.29
  142.6 23.3 %all-gather.12.cloned.1.call-done = f32[4,16,64,128]{3,2,1,0:T(8,128)} async-done(((f32[1,16,64,128]{3,2,1,0:T(8,128)}), f32[4,16,64,128]{3,2,1,0:T(8,128)}) %all-gather.12.cloned.1.call-update) | async-done | bytes 2097168 | tf_op jit(solution)/shard_map/all_gather | solution.py:24
  180.4 5.5 multiply_reduce_fusion.6
  188.4 5.9 multiply_reduce_fusion
  196.7 6.6 fusion.168
  220.0 46.4 %while.117 = (s32[]{:T(128)}, f32[1,16,64,128]{3,2,1,0:T(8,128)S(1)}, f32[2,1,256,256,16]{3,4,2,1,0:T(8,128)}, f32[2,1,128,256]{2,3,1,0:T(8,128)}, f32[2,1,256,1...) while((s32[]{:T(128)}, ...), condition=%wide.region_19.20_spmd.clone.clone, body=%wide.region_16.19_spmd.clone.clone.sunk | while | flops 912007232 | bytes 91645848 | solution.py:69
  225.1 6.2 multiply_dynamic-update-slice_fusion.4
  248.3 6.3 multiply_dynamic-update-slice_fusion.4
  275.5 5.1 fusion.218
  284.0 7.4 while.119
  295.2 106.7 %while.121 = (s32[]{:T(128)}, f32[16]{0:T(128)}, f32[1,16,64,128]{3,2,1,0:T(8,128)S(1)}, f32[2,1,256,16,64]{2,4,3,1,0:T(8,128)}, f32[2,1,256,128]{3,2,1,0:T(8,12...) while((s32[]{:T(128)}, f32[16]{0:T(128)}, ...), condition=%wide.region_32.33_spmd.clone.clone, body=%wide.region_20.32_spmd.clone.clone.sunk | while | flops 3434913792 | bytes 128233152 | solution.py:69
  295.3 6.7 constant_dynamic-slice_fusion.20
  304.4 11.3 fusion.331
  326.2 8.9 fusion.330
  348.5 6.7 constant_dynamic-slice_fusion.20
  357.6 11.3 fusion.331
  379.4 8.9 fusion.330
  411.6 6.8 fusion.222
  425.4 5.7 fusion.162
  431.2 9.9 all-reduce.15.cloned.1.call-done
  451.8 4.9 fusion.214
  463.5 247.3 %all-reduce.13.cloned.1.call-done = (f32[1024,1024]{1,0:T(8,128)}, f32[1024,1024]{1,0:T(8,128)}, f32[1024,16]{0,1:T(8,128)}, f32[1024,256]{1,0:T(8,128)}, f32[1024,1024]{1,0:T(8,128)}) async-done(((f32[1024,1024]{1,0:T(8,128)}, f32[1024,1024]{1,0:T(8,128)}, f32[1024,16]{0,1:T(8,128)}, f32[1024,256]{1,0:T(8,128)}, f32[1024,1024]{1,0:T(8,128)}), (f32[1024,1024]{1,0:T(8,128)}, f32[1024,1024]{1,0:T(8,128)}, ...) | async-done | bytes 13697040 | tf_op jit(solution)/shard_map/psum | solution.py:262
  713.2 10.1 reduce-scatter.3.cloned.1.call-done
  725.8 10.7 reduce-scatter.5.cloned.1.call-done
  739.5 17.0 %all-reduce.4 = (f32[512]{0:T(512)S(1)}, f32[4,1024]{1,0:T(4,128)S(1)}, f32[1024]{0:T(1024)S(1)}, f32[4,256]{1,0:T(4,128)S(1)}, f32[256]{0:T(256)S(1)}, /*index=...) all-reduce(f32[512]{0:T(512)S(1)} %get-tuple-element.1965, ...), channel_id=1, replica_groups=mesh['batch'=4,'seq'=4,'head'=2] {'batch'}, use_global_device_ids=true, to_apply=%region_39.40 | all-reduce | flops 7984 | bytes 63872 | tf_op jit(solution)/shard_map/psum | solution.py:262
  759.0 23.3 %all-reduce.2 = (f32[512]{0:T(512)}, f32[4,1024]{1,0:T(4,128)}, f32[1024]{0:T(1024)}, f32[4,256]{1,0:T(4,128)}, f32[256]{0:T(256)}, /*index=5*/f32[16]{0:T(128)}, f32[16]{0:T(128)}, f32[16]{0:T(128)}, f32[1024]{0:T(1024)}) all-reduce(f32[512]{0:T(512)S(1)} %get-tuple-element.2138, ...), channel_id=1, replica_groups=mesh['batch'=4,'seq'=4,'head'=2] {'seq'}, use_global_device_ids=true, to_apply=%region_40.41 | all-reduce | flops 7984 | bytes 63872 | tf_op jit(solution)/shard_map/psum | solution.py:261
  785.2 419.3 %all-reduce.11.cloned.1.call-done = (f32[1024,1024]{1,0:T(8,128)}, f32[1024,1024]{1,0:T(8,128)}, f32[1024,16]{0,1:T(8,128)}, f32[1024,256]{1,0:T(8,128)}, f32[1024,1024]{1,0:T(8,128)}) async-done(((f32[1024,1024]{1,0:T(8,128)}, f32[1024,1024]{1,0:T(8,128)}, f32[1024,16]{0,1:T(8,128)}, f32[1024,256]{1,0:T(8,128)}, f32[1024,1024]{1,0:T(8,128)}), (f32[1024,1024]{1,0:T(8,128)}, f32[1024,1024]{1,0:T(8,128)}, ...) | async-done | bytes 13697040 | tf_op jit(solution)/shard_map/psum | solution.py:261
  1204.6 4.9 copy.562
  (621 shorter events, 277.4 us)
Async XLA Ops:
  7.2 173.2 %copy-start = (bf16[1024,1024]{1,0:T(8,128)(2,1)S(1)}, bf16[1024,1024]{1,0:T(8,128)(2,1)}, u32[]{:S(2)}) copy-start(bf16[1024,1024]{1,0:T(8,128)(2,1)} %param.28) | copy-start | bytes 6291460
  7.2 14.1 %all-gather.8.cloned.1.call-start = ((), (), s32[]{:S(2)}) async-start(), calls=%async_computation.2 | async-start | bytes 1572864 | tf_op jit(solution)/shard_map/all_gather | solution.py:132
  7.9 158.0 %all-gather.12.cloned.1.call-start = ((), (), s32[]{:S(2)}) async-start(), calls=%async_computation.6 | async-start | bytes 2621440 | tf_op jit(solution)/shard_map/all_gather | solution.py:24
  10.7 169.7 %copy-start.54 = (f32[2,1,512]{2,1,0:T(1,128)}, f32[2,1,512]{2,1,0:T(1,128)S(1)}, u32[]{:S(2)}) copy-start(f32[2,1,512]{2,1,0:T(1,128)S(1)} %convert_element_type.86) | copy-start | bytes 12292
  12.7 23.3 %copy-start.88 = (f32[1,256]{1,0:T(1,128)}, f32[1,256]{1,0:T(1,128)S(1)}, u32[]{:S(2)}) copy-start(f32[1,256]{1,0:T(1,128)S(1)} %get-tuple-element.2211) | copy-start | bytes 3076
  12.7 23.3 %copy-start.90 = (f32[1,256]{1,0:T(1,128)}, f32[1,256]{1,0:T(1,128)S(1)}, u32[]{:S(2)}) copy-start(f32[1,256]{1,0:T(1,128)S(1)} %get-tuple-element.2212) | copy-start | bytes 3076
  12.7 23.3 %copy-start.92 = (f32[1,256]{1,0:T(1,128)}, f32[1,256]{1,0:T(1,128)S(1)}, u32[]{:S(2)}) copy-start(f32[1,256]{1,0:T(1,128)S(1)} %get-tuple-element.2213) | copy-start | bytes 3076
  12.7 23.3 %copy-start.94 = (f32[1,256]{1,0:T(1,128)}, f32[1,256]{1,0:T(1,128)S(1)}, u32[]{:S(2)}) copy-start(f32[1,256]{1,0:T(1,128)S(1)} %get-tuple-element.2214) | copy-start | bytes 3076
  13.6 23.7 %copy-start.67 = (f32[1,1024]{1,0:T(1,128)}, f32[1,1024]{1,0:T(1,128)S(1)}, u32[]{:S(2)}) copy-start(f32[1,1024]{1,0:T(1,128)S(1)} %get-tuple-element.2207) | copy-start | bytes 12292
  13.6 23.7 %copy-start.69 = (f32[1,1024]{1,0:T(1,128)}, f32[1,1024]{1,0:T(1,128)S(1)}, u32[]{:S(2)}) copy-start(f32[1,1024]{1,0:T(1,128)S(1)} %get-tuple-element.2208) | copy-start | bytes 12292
  13.6 23.7 %copy-start.71 = (f32[1,1024]{1,0:T(1,128)}, f32[1,1024]{1,0:T(1,128)S(1)}, u32[]{:S(2)}) copy-start(f32[1,1024]{1,0:T(1,128)S(1)} %get-tuple-element.2209) | copy-start | bytes 12292
  13.6 23.7 %copy-start.73 = (f32[1,1024]{1,0:T(1,128)}, f32[1,1024]{1,0:T(1,128)S(1)}, u32[]{:S(2)}) copy-start(f32[1,1024]{1,0:T(1,128)S(1)} %get-tuple-element.2210) | copy-start | bytes 12292
  23.0 157.4 %copy-start.61 = (f32[512]{0:T(512)}, f32[512]{0:T(512)S(1)}, u32[]{:S(2)}) copy-start(f32[512]{0:T(512)S(1)} %add_rsqrt_fusion.1) | copy-start | bytes 6148
  24.9 11.2 copy-start.31
  24.9 9.9 copy-start.75
  24.9 11.1 collective-permute-start.1
  31.4 5.8 collective-permute-start
  50.0 72.3 %copy-start.99 = (f32[16]{0:T(128)S(1)}, f32[16]{0:T(128)}, u32[]{:S(2)}) copy-start(f32[16]{0:T(128)} %param.38) | copy-start | bytes 196
  120.8 67.6 %all-gather.10.cloned.1.call-start = ((), (), s32[]{:S(2)}) async-start(), calls=%async_computation.4 | async-start | bytes 1572864 | tf_op jit(solution)/shard_map/all_gather | solution.py:133
  121.5 162.5 %all-gather.14.cloned.1.call-start = ((), (), s32[]{:S(2)}) async-start(), calls=%async_computation.7 | async-start | bytes 2621440 | tf_op jit(solution)/shard_map/all_gather | solution.py:24
  213.4 227.6 %all-reduce.15.cloned.1.call-start = ((), (), s32[]{:S(2)}) async-start(), calls=%async_computation.10 | async-start | bytes 1048576 | tf_op jit(solution)/shard_map/psum | solution.py:213
  326.2 11.3 copy-start.85
  379.4 11.3 copy-start.85
  419.8 5.6 collective-permute-start.2
  421.3 289.5 %all-reduce.13.cloned.1.call-start = ((), (), s32[]{:S(2)}) async-start(), calls=%async_computation.9 | async-start | bytes 27394048 | tf_op jit(solution)/shard_map/psum | solution.py:262
  421.3 19.8 %copy-start.81 = (f32[1,3,256]{2,1,0:T(4,128)S(1)}, f32[1,3,256]{2,1,0:T(4,128)}, u32[]{:S(2)}) copy-start(f32[1,3,256]{2,1,0:T(4,128)} %copy-done.80) | copy-start | bytes 9220
  443.8 5.5 collective-permute-start.3
  451.1 272.1 %reduce-scatter.3.cloned.1.call-start = ((), (), s32[]{:S(2)}) async-start(), calls=%async_computation.3 | async-start | bytes 3145728 | tf_op jit(solution)/shard_map/reduce_scatter | solution.py:187
  456.7 279.8 %reduce-scatter.5.cloned.1.call-start = ((), (), s32[]{:S(2)}) async-start(), calls=%async_computation.5 | async-start | bytes 3145728 | tf_op jit(solution)/shard_map/reduce_scatter | solution.py:249
  463.4 741.2 %all-reduce.11.cloned.1.call-start = ((), (), s32[]{:S(2)}) async-start(), calls=%async_computation.8 | async-start | bytes 27394048 | tf_op jit(solution)/shard_map/psum | solution.py:261
  725.8 13.7 %copy-start.98 = (f32[1024]{0:T(1024)S(1)}, f32[1024]{0:T(1024)}, u32[]{:S(2)}) copy-start(f32[1024]{0:T(1024)} %get-tuple-element.1963) | copy-start | bytes 12292
  736.5 45.8 %copy-start.36 = (f32[512,512]{1,0:T(8,128)S(1)}, f32[512,512]{1,0:T(8,128)}, u32[]{:S(2)}) copy-start(f32[512,512]{1,0:T(8,128)} %reduce-scatter.5.cloned.1.call-done) | copy-start | bytes 3145732
  (128 other events, 564.9 us)
Sparse Core Ops, SparseCore 0:
  9.5 11.7 all-gather.7
  120.9 44.9 all-gather.11
  167.5 7.8 all-gather.9
  213.6 44.5 all-gather.13
  421.4 19.6 all-reduce.14
  451.3 259.4 all-reduce.12
  713.0 10.2 reduce-scatter.2
  725.5 10.8 reduce-scatter.4
  739.6 464.9 all-reduce.10
